TPU v7x, 32 devices: a whole 2x2x4 slice. The times are simulated.
32 devices in a mesh: shot: 8 (over y, x, core), depth: 4 (over z).
Axes of the slice: x: 2, y: 2, z: 4, core: 2. Of those that a mesh axis runs over, the one named last changes fastest.
Arguments:
- probes: bfloat16 [8, 64, 128, 128], P('shot', None, 'depth'), may hold values from -6 to 6
- courant: float32 [128, 128], P('depth'), may hold values from 0.1 to 0.45
- sketches: float32 [8, 128, 64], replicated, may hold values from -0.5 to 0.5
Outputs:
- basis: float32 [64, 128, 128], P(None, 'depth')
- cores: float32 [8, 64, 64], P('shot')
All inputs are finite; a program needn't handle non-finite values.
Results may differ from a plain program's by a relative error of at most 0.0003.
Values may be sent and summed in bfloat16 or wider, within the bound.
A program may use at most 64 MiB of HBM per device.

v0:
```python
import math

import jax
import jax.numpy as jnp
from jax import lax
from jax.sharding import PartitionSpec as P

STEPS = 4


def with_halo(shard, sides, width):
    for axis, dim in sides:
        size, length = (lax.axis_size(axis), shard.shape[dim])
        up = [(i, (i + 1) % size) for i in range(size - 1)]
        down = [(j, i) for i, j in up]
        last = lax.slice_in_dim(shard, length - width, length, axis=dim)
        first = lax.slice_in_dim(shard, 0, width, axis=dim)
        before = lax.ppermute(last, axis, up)
        after = lax.ppermute(first, axis, down)
        shard = jnp.concatenate([before, shard, after], axis=dim)
    return shard


def swapped(shard, axis, distance):
    return lax.ppermute(shard, axis, [(i, i ^ 1 << distance) for i in range(lax.axis_size(axis))])


def laplacian(padded, current):
    return (
        padded[:, 2:, 1:-1]
        + padded[:, :-2, 1:-1]
        + padded[:, 1:-1, 2:]
        + padded[:, 1:-1, :-2]
        - 4.0 * current
    )


def wave_deep(local_probes, courant):
    rows = courant.shape[0]
    wide_probes = with_halo(local_probes, (("depth", 1),), STEPS).astype(jnp.float32)
    wide_speed = with_halo(courant, (("depth", 0),), STEPS)
    global_row = (
        lax.axis_index("depth") * rows - STEPS + jnp.arange(rows + 2 * STEPS, dtype=jnp.int32)
    )
    inside = ((global_row >= 0) & (global_row < rows * lax.axis_size("depth"))).astype(jnp.float32)[
        :, None
    ]
    earlier = wide_probes
    current = wide_probes
    for repeat in range(STEPS):
        padded = jnp.pad(current, ((0, 0), (1, 1), (1, 1)))
        laplace = laplacian(padded, current)
        earlier, current = (current, (2.0 * current - earlier + wide_speed * laplace) * inside)
    return current[:, STEPS : STEPS + rows]


def orthonormal(matrix):
    gram = lax.psum(jnp.dot(matrix, matrix.T, precision=lax.Precision.HIGHEST), "depth")
    lower_factor = jnp.linalg.cholesky(gram)
    return lax.linalg.triangular_solve(lower_factor, matrix, left_side=True, lower=True)


def body(probes, courant, sketches):
    local_probes = probes[0]
    field = wave_deep(local_probes, courant)
    rank = field.shape[0]
    flattened = field.reshape(rank, -1)
    factor = orthonormal(flattened)
    position = lax.axis_index("shot")
    for height in range(lax.axis_size("shot").bit_length() - 1):
        stride = 2**height
        block_start = position // (2 * stride) * (2 * stride)
        sketch = lax.dynamic_index_in_dim(sketches, block_start + stride - 1, 0, keepdims=False)
        partner = swapped(factor, "shot", height)
        upper_bit = position // stride % 2 == 1
        low_factor = jnp.where(upper_bit, partner, factor)
        high_factor = jnp.where(upper_bit, factor, partner)
        mixed = jnp.dot(sketch[:rank].T, low_factor, precision=lax.Precision.HIGHEST) + jnp.dot(
            sketch[rank:].T, high_factor, precision=lax.Precision.HIGHEST
        )
        factor = orthonormal(mixed)
    partial_cores = (
        jnp.dot(factor, flattened.T, precision=lax.Precision.HIGHEST) / math.sqrt(rank)
    )[None]
    cores = lax.psum(partial_cores, "depth")
    return (factor.reshape(field.shape), cores)


def solution(mesh):
    placed = (P("shot", None, "depth", None), P("depth", None), P())
    return jax.shard_map(
        body,
        mesh=mesh,
        in_specs=placed,
        out_specs=(P(None, "depth", None), P("shot", None, None)),
        check_vma=False,
    )
```

profile of v0, /device:TPU:0, one launch (start us, length us, event | category | flops | bytes accessed | tf_op | source)
XLA Modules:
  0.0 223.0 jit_solution(9057073619201705798)
XLA Ops:
  0.7 1.3 copy.40
  2.0 5.0 %collective-permute-start = (bf16[64,4,128]{2,0,1:T(8,128)(2,1)S(1)}, bf16[64,4,128]{2,0,1:T(8,128)(2,1)S(1)}, u32[]{:S(2)}, u32[]{:S(2)}) collective-permute-start(bf16[64,4,128]{2,0,1:T(8,128)(2,1)S(1)} %get-tuple-element.4), channel_id=1, source_target_pairs={{0,1},{1,2},{2,3},{4,5},{5,6},{6,7},{8,9},{9,10},{10,11},{12,13},{... | collective-permute-start | bytes 196616 | tf_op jit(solution)/shard_map/ppermute | solution.py:18
  6.9 1.3 collective-permute-start.1
  8.3 4.5 %collective-permute-start.2 = (f32[4,128]{1,0:T(4,128)S(1)}, f32[4,128]{1,0:T(4,128)S(1)}, u32[]{:S(2)}, u32[]{:S(2)}) collective-permute-start(f32[4,128]{1,0:T(4,128)S(1)} %get-tuple-element.6), channel_id=1, source_target_pairs={{0,1},{1,2},{2,3},{4,5},{5,6},{6,7},{8,9},{9,10},{10,11},{12,13},{... | collective-permute-start | bytes 6152 | tf_op jit(solution)/shard_map/ppermute | solution.py:18
  12.8 1.3 collective-permute-start.3
  14.1 4.2 %collective-permute-done.3 = f32[4,128]{1,0:T(4,128)S(1)} collective-permute-done((f32[4,128]{1,0:T(4,128)S(1)}, f32[4,128]{1,0:T(4,128)S(1)}, u32[]{:S(2)}, u32[]{:S(2)}) %collective-permute-start.3) | collective-permute-done | bytes 2080 | tf_op jit(solution)/shard_map/ppermute | solution.py:19
  20.0 1.6 fusion.20
  23.5 17.4 %psum.35 = f32[64,64]{0,1:T(8,128)S(1)} all-reduce(f32[64,64]{0,1:T(8,128)S(1)} %convolution_bitcast_fusion), channel_id=1, replica_groups=mesh['shot'=8,'depth'=4] {'depth'}, use_global_device_ids=true, to_apply=%region_0.1 | all-reduce | flops 4096 | bytes 32768 | tf_op jit(solution)/shard_map/psum | solution.py:58
  41.0 5.8 %cholesky.74 = f32[64,64]{1,0:T(8,128)S(1)} custom-call(f32[64,64]{1,0:T(8,128)S(1)} %fusion.64), custom_call_target="Cholesky" | custom-call | tf_op jit(solution)/shard_map/jit(cholesky)/cholesky | solution.py:59
  48.2 4.9 %custom-call.8 = f32[1,64,64]{1,2,0:T(8,128)S(1)} custom-call(f32[1,64,64]{2,1,0:T(8,128)S(1)} %fusion.50), custom_call_target="InvertDiagBlocksLowerTriangular" | custom-call | tf_op jit(solution)/shard_map/triangular_solve/custom-call.0 | solution.py:60
  54.3 2.7 %collective-permute-done.4 = f32[64,4096]{1,0:T(8,128)} collective-permute-done((f32[64,4096]{1,0:T(8,128)S(1)}, f32[64,4096]{1,0:T(8,128)}, u32[]{:S(2)}, u32[]{:S(2)}) %collective-permute-start.4) | collective-permute-done | bytes 1048608 | tf_op jit(solution)/shard_map/ppermute | solution.py:25
  57.0 2.3 %fusion.38 = f32[64,4096]{1,0:T(8,128)S(1)} fusion(f32[64,4096]{1,0:T(8,128)S(1)} %fusion.30, f32[64,4096]{1,0:T(8,128)} %collective-permute-done.4, pred[]{:T(512)S(6)} %eq.15, f32[8,128,64]{1,2,0:T(8,128)S(1)} %copy-done, s32[]{:T(128)S(6)} %select_n.82, s32[]{:T(128)S(6)} %add.171), kind=kOutput, calls=%fused_computation.60 | convolution fusion | flops 201588736 | bytes 3178505 | tf_op jit(solution)/shard_map/dot_general | solution.py:78
  59.4 2.2 convolution_add_fusion.2
  62.6 16.1 %psum.36 = f32[64,64]{0,1:T(8,128)S(1)} all-reduce(f32[64,64]{0,1:T(8,128)S(1)} %fusion.79), channel_id=1, replica_groups=mesh['shot'=8,'depth'=4] {'depth'}, use_global_device_ids=true, to_apply=%region_3.6 | all-reduce | flops 4096 | bytes 32768 | tf_op jit(solution)/shard_map/psum | solution.py:58
  78.8 5.8 %cholesky.85 = f32[64,64]{1,0:T(8,128)S(1)} custom-call(f32[64,64]{1,0:T(8,128)S(1)} %fusion.62), custom_call_target="Cholesky" | custom-call | tf_op jit(solution)/shard_map/jit(cholesky)/cholesky | solution.py:59
  86.0 4.9 %custom-call.9 = f32[1,64,64]{1,2,0:T(8,128)S(1)} custom-call(f32[1,64,64]{2,1,0:T(8,128)S(1)} %fusion.51), custom_call_target="InvertDiagBlocksLowerTriangular" | custom-call | tf_op jit(solution)/shard_map/triangular_solve/custom-call.0 | solution.py:60
  90.9 2.0 fusion.60
  92.9 1.5 collective-permute-start.5
  94.4 19.0 %collective-permute-done.5 = f32[64,4096]{1,0:T(8,128)S(1)} collective-permute-done((f32[64,4096]{1,0:T(8,128)}, f32[64,4096]{1,0:T(8,128)S(1)}, u32[]{:S(2)}, u32[]{:S(2)}) %collective-permute-start.5) | collective-permute-done | bytes 1048608 | tf_op jit(solution)/shard_map/ppermute | solution.py:25
  115.5 2.2 convolution_add_fusion.1
  118.7 17.4 %psum.37 = f32[64,64]{0,1:T(8,128)S(1)} all-reduce(f32[64,64]{0,1:T(8,128)S(1)} %fusion.80), channel_id=1, replica_groups=mesh['shot'=8,'depth'=4] {'depth'}, use_global_device_ids=true, to_apply=%region_4.7 | all-reduce | flops 4096 | bytes 32768 | tf_op jit(solution)/shard_map/psum | solution.py:58
  136.2 5.8 %cholesky.96 = f32[64,64]{1,0:T(8,128)S(1)} custom-call(f32[64,64]{1,0:T(8,128)S(1)} %fusion.59), custom_call_target="Cholesky" | custom-call | tf_op jit(solution)/shard_map/jit(cholesky)/cholesky | solution.py:59
  143.4 4.9 %custom-call.10 = f32[1,64,64]{1,2,0:T(8,128)S(1)} custom-call(f32[1,64,64]{2,1,0:T(8,128)S(1)} %fusion.52), custom_call_target="InvertDiagBlocksLowerTriangular" | custom-call | tf_op jit(solution)/shard_map/triangular_solve/custom-call.0 | solution.py:60
  148.3 2.0 fusion.57
  150.3 1.5 collective-permute-start.6
  151.8 14.4 %collective-permute-done.6 = f32[64,4096]{1,0:T(8,128)S(1)} collective-permute-done((f32[64,4096]{1,0:T(8,128)}, f32[64,4096]{1,0:T(8,128)S(1)}, u32[]{:S(2)}, u32[]{:S(2)}) %collective-permute-start.6) | collective-permute-done | bytes 1048608 | tf_op jit(solution)/shard_map/ppermute | solution.py:25
  168.4 2.2 convolution_add_fusion
  171.6 16.3 %psum.38 = f32[64,64]{0,1:T(8,128)S(1)} all-reduce(f32[64,64]{0,1:T(8,128)S(1)} %fusion.81), channel_id=1, replica_groups=mesh['shot'=8,'depth'=4] {'depth'}, use_global_device_ids=true, to_apply=%region_5.8 | all-reduce | flops 4096 | bytes 32768 | tf_op jit(solution)/shard_map/psum | solution.py:58
  187.9 5.8 %cholesky.107 = f32[64,64]{1,0:T(8,128)S(1)} custom-call(f32[64,64]{1,0:T(8,128)S(1)} %fusion.56), custom_call_target="Cholesky" | custom-call | tf_op jit(solution)/shard_map/jit(cholesky)/cholesky | solution.py:59
  195.1 4.9 %custom-call.11 = f32[1,64,64]{1,2,0:T(8,128)S(1)} custom-call(f32[1,64,64]{2,1,0:T(8,128)S(1)} %fusion.53), custom_call_target="InvertDiagBlocksLowerTriangular" | custom-call | tf_op jit(solution)/shard_map/triangular_solve/custom-call.0 | solution.py:60
  203.0 17.6 %psum.39 = f32[1,64,64]{2,1,0:T(8,128)} all-reduce(f32[1,64,64]{2,1,0:T(8,128)S(1)} %fusion.28), channel_id=1, replica_groups=mesh['shot'=8,'depth'=4] {'depth'}, use_global_device_ids=true, to_apply=%region_6.9 | all-reduce | flops 4096 | bytes 32768 | tf_op jit(solution)/shard_map/psum | solution.py:85
  220.7 2.4 %copy.30 = f32[8,8,32,128]{3,2,1,0:T(8,128)} copy(f32[8,8,32,128]{3,1,2,0:T(8,128)} %bitcast.85) | data formatting | bytes 2097152
  (53 shorter events, 20.4 us)
Async XLA Ops:
  0.6 56.4 %copy-start = (f32[8,128,64]{1,2,0:T(8,128)S(1)}, f32[8,128,64]{1,2,0:T(8,128)}, u32[]{:S(2)}) copy-start(f32[8,128,64]{1,2,0:T(8,128)} %param.8) | copy-start | bytes 786436
  0.6 7.6 %copy-start.5 = (f32[32,128]{1,0:T(8,128)S(1)}, f32[32,128]{1,0:T(8,128)}, u32[]{:S(2)}) copy-start(f32[32,128]{1,0:T(8,128)} %param.7) | copy-start | bytes 49156
  2.0 16.3 %collective-permute-start = (bf16[64,4,128]{2,0,1:T(8,128)(2,1)S(1)}, bf16[64,4,128]{2,0,1:T(8,128)(2,1)S(1)}, u32[]{:S(2)}, u32[]{:S(2)}) collective-permute-start(bf16[64,4,128]{2,0,1:T(8,128)(2,1)S(1)} %get-tuple-element.4), channel_id=1, source_target_pairs={{0,1},{1,2},{2,3},{4,5},{5,6},{6,7},{8,9},{9,10},{10,11},{12,13},{... | collective-permute-start | bytes 196616 | tf_op jit(solution)/shard_map/ppermute | solution.py:18
  6.9 11.4 %collective-permute-start.1 = (bf16[64,4,128]{2,0,1:T(8,128)(2,1)S(1)}, bf16[64,4,128]{2,0,1:T(8,128)(2,1)S(1)}, u32[]{:S(2)}, u32[]{:S(2)}) collective-permute-start(bf16[64,4,128]{2,0,1:T(8,128)(2,1)S(1)} %get-tuple-element.5), channel_id=1, source_target_pairs={{1,0},{2,1},{3,2},{5,4},{6,5},{7,6},{9,8},{10,9},{11,10},{13,12},{... | collective-permute-start | bytes 196616 | tf_op jit(solution)/shard_map/ppermute | solution.py:19
  8.3 5.9 %collective-permute-start.2 = (f32[4,128]{1,0:T(4,128)S(1)}, f32[4,128]{1,0:T(4,128)S(1)}, u32[]{:S(2)}, u32[]{:S(2)}) collective-permute-start(f32[4,128]{1,0:T(4,128)S(1)} %get-tuple-element.6), channel_id=1, source_target_pairs={{0,1},{1,2},{2,3},{4,5},{5,6},{6,7},{8,9},{9,10},{10,11},{12,13},{... | collective-permute-start | bytes 6152 | tf_op jit(solution)/shard_map/ppermute | solution.py:18
  12.8 5.5 %collective-permute-start.3 = (f32[4,128]{1,0:T(4,128)S(1)}, f32[4,128]{1,0:T(4,128)S(1)}, u32[]{:S(2)}, u32[]{:S(2)}) collective-permute-start(f32[4,128]{1,0:T(4,128)S(1)} %get-tuple-element.7), channel_id=1, source_target_pairs={{1,0},{2,1},{3,2},{5,4},{6,5},{7,6},{9,8},{10,9},{11,10},{13,12},{... | collective-permute-start | bytes 6152 | tf_op jit(solution)/shard_map/ppermute | solution.py:19
  54.2 2.9 %copy-start.1 = (f32[64,4096]{1,0:T(8,128)}, f32[64,4096]{1,0:T(8,128)S(1)}, u32[]{:S(2)}) copy-start(f32[64,4096]{1,0:T(8,128)S(1)} %fusion.30) | copy-start | bytes 3145732
  54.2 2.9 %collective-permute-start.4 = (f32[64,4096]{1,0:T(8,128)S(1)}, f32[64,4096]{1,0:T(8,128)}, u32[]{:S(2)}, u32[]{:S(2)}) collective-permute-start(f32[64,4096]{1,0:T(8,128)S(1)} %fusion.30), channel_id=1, source_target_pairs={{0,4},{4,0},{8,12},{12,8},{16,20},{20,16},{24,28},{28,24},{1,5},{5... | collective-permute-start | bytes 3145736 | tf_op jit(solution)/shard_map/ppermute | solution.py:25
  92.9 20.5 %collective-permute-start.5 = (f32[64,4096]{1,0:T(8,128)}, f32[64,4096]{1,0:T(8,128)S(1)}, u32[]{:S(2)}, u32[]{:S(2)}) collective-permute-start(f32[64,4096]{1,0:T(8,128)} %fusion.60), channel_id=1, source_target_pairs={{0,8},{4,12},{8,0},{12,4},{16,24},{20,28},{24,16},{28,20},{1,9},{5... | collective-permute-start | bytes 3145736 | tf_op jit(solution)/shard_map/ppermute | solution.py:25
  113.4 1.0 copy-start.4
  150.3 16.0 %collective-permute-start.6 = (f32[64,4096]{1,0:T(8,128)}, f32[64,4096]{1,0:T(8,128)S(1)}, u32[]{:S(2)}, u32[]{:S(2)}) collective-permute-start(f32[64,4096]{1,0:T(8,128)} %fusion.57), channel_id=1, source_target_pairs={{0,16},{4,20},{8,24},{12,28},{16,0},{20,4},{24,8},{28,12},{1,17},{... | collective-permute-start | bytes 3145736 | tf_op jit(solution)/shard_map/ppermute | solution.py:25
  166.3 1.0 copy-start.3
  201.1 1.0 copy-start.2
where the time goes:
time: 225 us; the launch traced here: 223 us
  blocking collectives  84.8 us (38%)
  other arithmetic  52.5 us (23%)
  waiting for transfers between devices  40.4 us (18%)
  matrix products  22.2 us (10%)
  starting transfers between devices  15.2 us (7%)
  local copies, waits for them, and re-layouts  6.97 us (3%)
    psum x4, blocking collectives, orthonormal(): lax.psum(jnp.dot(matrix, matrix.T, precision=lax.Precision.HIGHEST), 'dep...  67.2 us
    ppermute x3, waiting for transfers between devices, swapped(): lax.ppermute(shard, axis, [(i, i ^ 1 << distance) for i in range(lax.axis...  36.2 us
    another operation x12, other arithmetic, orthonormal(): lower_factor = jnp.linalg.cholesky(gram)  26.1 us
    another operation x8, other arithmetic, orthonormal(): lax.linalg.triangular_solve(lower_factor, matrix, left_side=True, lower=T...  22.2 us
    psum x1, blocking collectives, body(): cores = lax.psum(partial_cores, 'depth')  17.6 us
    ppermute x2, starting transfers between devices, with_halo(): before = lax.ppermute(last, axis, up)  9.51 us
    unnamed x14, local copies, waits for them, and re-layouts  6.66 us
    dot_general x3, matrix products, body(): jnp.dot(sketch[:rank].T, low_factor, precision=lax.Precision.HIGHEST)  6.66 us
  transfers between devices with their start and end apart: 7, of which 4 were waited for; matrix products, arithmetic and copies ran while one was open for 0% of the time, Pallas kernels for 0%

commit v1 on v0

v1 whole, which is shorter than its diff:
```python
import functools
import math

import jax
import jax.numpy as jnp
from jax import lax
from jax.experimental import pallas as pl
from jax.experimental.pallas import tpu as pltpu
from jax.sharding import PartitionSpec as P

STEPS = 4
MESH = pl.DeviceIdType.MESH
HI = lax.Precision.HIGHEST
NN = (((1,), (0,)), ((), ()))
NT = (((1,), (1,)), ((), ()))
TN = (((0,), (0,)), ((), ()))
PIECES = 4


def mm(a, b, dims=NN):
    return lax.dot_general(a, b, dims, precision=HI, preferred_element_type=jnp.float32)


def inverse_factor(gram):
    n = gram.shape[0]
    rows = lax.broadcasted_iota(jnp.int32, (n, 1), 0)
    eye = (
        lax.broadcasted_iota(jnp.int32, (n, n), 0) == lax.broadcasted_iota(jnp.int32, (n, n), 1)
    ).astype(jnp.float32)
    a = jnp.concatenate([gram, eye], axis=1)
    blocks = [a[8 * b : 8 * b + 8] for b in range(n // 8)]
    for k in range(n - 1):
        b0, r = divmod(k, 8)
        row = blocks[b0][r : r + 1]
        row = row * (1.0 / row[:, k : k + 1])
        for b in range((k + 1) // 8, n // 8):
            col = blocks[b][:, k : k + 1]
            if b == b0:
                col = jnp.where(rows[:8] > r, col, 0.0)
            blocks[b] = blocks[b] - col * row
    a = jnp.concatenate(blocks, axis=0)
    pivots = jnp.sum(a[:, :n] * eye, axis=1, keepdims=True)
    return a[:, n:] * (1.0 / jnp.sqrt(pivots))


def kernel(
    depths,
    levels,
    probes,
    speed,
    sketches,
    basis,
    cores,
    halo,
    wide_speed,
    field_a,
    field_b,
    pairs,
    sums,
    sums_in,
    halo_send,
    halo_recv,
    speed_send,
    speed_recv,
    pair_send,
    pair_recv,
    fwd_send,
    fwd_recv,
    sum_send,
    sum_recv,
):
    rows, rank, cells = probes.shape
    shot = lax.axis_index("shot")
    depth = lax.axis_index("depth")
    low_end = depth == 0
    high_end = depth == depths - 1

    def bit(h):
        return lax.rem(shot // (2**h), 2)

    def peer(h):
        return shot + 2**h - 2 ** (h + 1) * bit(h)

    barrier = pltpu.get_barrier_semaphore()
    for h in range(levels):
        pl.semaphore_signal(barrier, inc=1, device_id=(peer(h), depth), device_id_type=MESH)
    for j in range(1, depths):
        other = lax.rem(depth + j, depths)
        pl.semaphore_signal(barrier, inc=1, device_id=(shot, other), device_id_type=MESH)
    pl.semaphore_wait(barrier, levels + depths - 1)

    def halo_copies(side):
        to = depth + 1 if side == 0 else depth - 1
        rows_out = pl.ds(rows - STEPS, STEPS) if side == 0 else pl.ds(0, STEPS)
        first = pltpu.make_async_remote_copy(
            src_ref=probes.at[rows_out],
            dst_ref=halo.at[side],
            send_sem=halo_send.at[side],
            recv_sem=halo_recv.at[side],
            device_id=(shot, to),
            device_id_type=MESH,
        )
        at = 0 if side == 0 else STEPS + rows
        second = pltpu.make_async_remote_copy(
            src_ref=speed.at[rows_out],
            dst_ref=wide_speed.at[pl.ds(at, STEPS)],
            send_sem=speed_send.at[side],
            recv_sem=speed_recv.at[side],
            device_id=(shot, to),
            device_id_type=MESH,
        )
        return first, second

    @pl.when(depth < depths - 1)
    def _():
        for c in halo_copies(0):
            c.start()

    @pl.when(depth > 0)
    def _():
        for c in halo_copies(1):
            c.start()

    @pl.loop(0, rows)
    def _(d):
        field_a[STEPS + d] = probes[d].astype(jnp.float32)

    wide_speed[STEPS : STEPS + rows] = speed[...]

    @pl.when(depth > 0)
    def _():
        for c in halo_copies(0):
            c.wait_recv()
        field_a[0:STEPS] = halo[0].astype(jnp.float32)

    @pl.when(depth == 0)
    def _():
        field_a[0:STEPS] = jnp.zeros((STEPS, rank, cells), jnp.float32)
        wide_speed[0:STEPS] = jnp.zeros((STEPS, cells), jnp.float32)

    @pl.when(depth < depths - 1)
    def _():
        for c in halo_copies(1):
            c.wait_recv()
        field_a[STEPS + rows : 2 * STEPS + rows] = halo[1].astype(jnp.float32)

    @pl.when(depth == depths - 1)
    def _():
        field_a[STEPS + rows : 2 * STEPS + rows] = jnp.zeros((STEPS, rank, cells), jnp.float32)
        wide_speed[STEPS + rows : 2 * STEPS + rows] = jnp.zeros((STEPS, cells), jnp.float32)

    lane = lax.broadcasted_iota(jnp.int32, (rank, cells), 1)
    not_first = lane > 0
    not_last = lane < cells - 1
    me = bit(0)
    mine = pl.ds(pl.multiple_of(me * rank, rank), rank)

    def update(d, source, older):
        u = source[d]
        left = jnp.where(not_first, pltpu.roll(u, 1, 1), 0.0)
        right = jnp.where(not_last, pltpu.roll(u, cells - 1, 1), 0.0)
        laplace = source[d + 1] + source[d - 1] + right + left - 4.0 * u
        return 2.0 * u - older + wide_speed[pl.ds(d, 1)] * laplace

    for step in range(STEPS):
        source, target = (field_a, field_b) if step % 2 == 0 else (field_b, field_a)
        last = step == STEPS - 1

        @pl.loop(step + 1, 2 * STEPS + rows - step - 1)
        def _(d):
            older = source[d] if step == 0 else target[d]
            new = update(d, source, older)
            if last:
                pairs[0, d - STEPS, mine] = new
            else:
                target[d] = new

    def pair_copy(h):
        own = pl.ds(pl.multiple_of(bit(h) * rank, rank), rank)
        return [
            pltpu.make_async_remote_copy(
                src_ref=pairs.at[h, :, own],
                dst_ref=pairs.at[h, :, own],
                send_sem=pair_send.at[h, 0],
                recv_sem=pair_recv.at[h, 0],
                device_id=(peer(h), depth),
                device_id_type=MESH,
            )
        ]

    for c in pair_copy(0):
        c.start()
    for c in pair_copy(0):
        c.wait()

    def gram_body(d, total):
        x = pairs[0, d]
        return total + mm(x, x, NT)

    zero = jnp.zeros((2 * rank, 2 * rank), jnp.float32)
    gram = lax.fori_loop(0, rows, gram_body, zero)

    def sum_copy(h, j):
        other = lax.rem(depth + j, depths)
        size = 2 * rank if h == 0 else rank
        return pltpu.make_async_remote_copy(
            src_ref=sums.at[h, pl.ds(0, size)],
            dst_ref=sums_in.at[h, depth, pl.ds(0, size)],
            send_sem=sum_send.at[h, j],
            recv_sem=sum_recv.at[h, j],
            device_id=(shot, other),
            device_id_type=MESH,
        )

    def depth_sum(h, value):
        size = value.shape[0]
        sums[h, 0:size] = value
        for j in range(1, depths):
            sum_copy(h, j).start()
        for j in range(1, depths):
            sum_copy(h, j).wait()
        total = None
        for j in range(depths):
            part = jnp.where(depth == j, value, sums_in[h, j, 0:size])
            total = part if total is None else total + part
        return total

    for h in range(levels):
        sums_in[h, depth] = jnp.zeros((2 * rank, 2 * rank), jnp.float32)
    gram = depth_sum(0, gram)

    low = inverse_factor(gram[:rank, :rank])
    high = inverse_factor(gram[rank:, rank:])
    sketch = sketches[shot // 2 * 2]
    mixer = jnp.concatenate(
        [mm(sketch[:rank], low, TN), mm(sketch[rank:], high, TN)], axis=1
    )
    carried = mm(mixer, gram)
    inverse = inverse_factor(mm(carried, mixer, NT))
    mixer = mm(inverse, mixer)
    carried = mm(inverse, carried)
    projected = jnp.where(me == 0, carried[:, :rank], carried[:, rank:])

    for h in range(1, levels):
        own_bit = bit(h)
        own = pl.ds(pl.multiple_of(own_bit * rank, rank), rank)

        @pl.loop(0, rows)
        def _(d):
            pairs[h, d, own] = mm(mixer, pairs[h - 1, d])

        per = rows // 2 // PIECES
        half = rows // 2

        def piece_copy(i):
            at = pl.ds(me * half + i * per, per)
            return pltpu.make_async_remote_copy(
                src_ref=pairs.at[h, at, own],
                dst_ref=pairs.at[h, at, own],
                send_sem=pair_send.at[h, i],
                recv_sem=pair_recv.at[h, i],
                device_id=(peer(h), depth),
                device_id_type=MESH,
            )

        got = pl.ds(pl.multiple_of((1 - own_bit) * rank, rank), rank)

        def forward_copy(i):
            at = pl.ds(me * half + i * per, per)
            return pltpu.make_async_remote_copy(
                src_ref=pairs.at[h, at, got],
                dst_ref=pairs.at[h, at, got],
                send_sem=fwd_send.at[h, i],
                recv_sem=fwd_recv.at[h, i],
                device_id=(peer(0), depth),
                device_id_type=MESH,
            )

        for i in range(PIECES):
            piece_copy(i).start()
        for i in range(PIECES):
            piece_copy(i).wait_recv()
            forward_copy(i).start()
        for i in range(PIECES):
            piece_copy(i).wait_send()
            forward_copy(i).wait()

        def cross_body(d, total):
            y = pairs[h, d]
            r = pairs[0, d, mine]
            return total + mm(y, jnp.concatenate([y[rank:], r], axis=0), NT)

        cross = lax.fori_loop(0, rows, cross_body, zero)
        value = jnp.concatenate(
            [
                cross[:rank, :rank],
                jnp.where(own_bit == 0, cross[rank:, rank:], cross[:rank, rank:]),
            ],
            axis=1,
        )
        value = depth_sum(h, value)
        stride = 2**h
        sketch = sketches[shot // (2 * stride) * (2 * stride) + stride - 1]
        top, bottom = sketch[:rank], sketch[rank:]
        across = value[:, :rank]
        mixed = mm(sketch, sketch, TN)
        mixed += mm(top, mm(across, bottom), TN) + mm(bottom, mm(across, top, TN), TN)
        inverse = inverse_factor(mixed)
        mixer = mm(inverse, sketch, NT)
        other = value[:, rank:]
        low_part = jnp.where(own_bit == 0, projected, other)
        high_part = jnp.where(own_bit == 0, other, projected)
        projected = mm(mixer, jnp.concatenate([low_part, high_part], axis=0))

    @pl.loop(0, rows)
    def _(d):
        basis[d] = mm(mixer, pairs[levels - 1, d])

    cores[...] = projected * (1.0 / math.sqrt(rank))

    @pl.when(depth < depths - 1)
    def _():
        for c in halo_copies(0):
            c.wait_send()

    @pl.when(depth > 0)
    def _():
        for c in halo_copies(1):
            c.wait_send()


def body(probes, courant, sketches):
    depths = lax.axis_size("depth")
    levels = lax.axis_size("shot").bit_length() - 1
    local = jnp.transpose(probes[0], (1, 0, 2))
    rows, rank, cells = local.shape
    f32 = jnp.float32
    vmem = pl.BlockSpec(memory_space=pltpu.VMEM)
    dma = pltpu.SemaphoreType.DMA
    basis, cores = pl.pallas_call(
        functools.partial(kernel, depths, levels),
        out_shape=(
            jax.ShapeDtypeStruct((rows, rank, cells), f32),
            jax.ShapeDtypeStruct((rank, rank), f32),
        ),
        in_specs=[vmem] * 3,
        out_specs=(vmem, vmem),
        scratch_shapes=[
            pltpu.VMEM((2, STEPS, rank, cells), jnp.bfloat16),
            pltpu.VMEM((rows + 2 * STEPS, cells), f32),
            pltpu.VMEM((rows + 2 * STEPS, rank, cells), f32),
            pltpu.VMEM((rows + 2 * STEPS, rank, cells), f32),
            pltpu.VMEM((levels, rows, 2 * rank, cells), f32),
            pltpu.VMEM((levels, 2 * rank, 2 * rank), f32),
            pltpu.VMEM((levels, depths, 2 * rank, 2 * rank), f32),
            dma((2,)),
            dma((2,)),
            dma((2,)),
            dma((2,)),
            dma((levels, PIECES)),
            dma((levels, PIECES)),
            dma((levels, PIECES)),
            dma((levels, PIECES)),
            dma((levels, depths)),
            dma((levels, depths)),
        ],
        compiler_params=pltpu.CompilerParams(
            collective_id=0, has_side_effects=True, vmem_limit_bytes=56 * 2**20
        ),
    )(local, courant, sketches)
    return (jnp.transpose(basis, (1, 0, 2)), cores[None])


def solution(mesh):
    placed = (P("shot", None, "depth", None), P("depth", None), P())
    return jax.shard_map(
        body,
        mesh=mesh,
        in_specs=placed,
        out_specs=(P(None, "depth", None), P("shot", None, None)),
        check_vma=False,
    )
```

time: 225 us -> 147 us (0.65)
  Pallas kernels: 0 us -> 140 us
  blocking collectives: 84.8 us -> 0 us
  other arithmetic: 52.5 us -> 0 us
  waiting for transfers between devices: 40.4 us -> 0 us
  matrix products: 22.2 us -> 0 us
  starting transfers between devices: 15.2 us -> 0 us
    pallas_call x0 -> x1, Pallas kernels: none -> 140 us  [body(): pl.pallas_call(functools.partial(kernel, depths, levels), out_shape=(jax....]
    psum x5 -> x0, blocking collectives: 84.8 us -> none  [the longest x4 67.2 us: orthonormal(): lax.psum(jnp.dot(matrix, matrix.T, precision=lax.Precision.HIGHEST), 'dep...]
    another operation x20 -> x0, other arithmetic: 48.3 us -> none  [the longest x12 26.1 us: orthonormal(): lower_factor = jnp.linalg.cholesky(gram)]
    ppermute x7 -> x0, waiting for transfers between devices: 40.4 us -> none  [the longest x3 36.2 us: swapped(): lax.ppermute(shard, axis, [(i, i ^ 1 << distance) for i in range(lax.axis...]
    dot_general x11 -> x0, matrix products: 16 us -> none  [the longest x3 6.66 us: body(): jnp.dot(sketch[:rank].T, low_factor, precision=lax.Precision.HIGHEST)]
    ppermute x7 -> x0, starting transfers between devices: 15.2 us -> none  [the longest x2 9.51 us: with_halo(): before = lax.ppermute(last, axis, up)]
    another operation x4 -> x0, matrix products: 6.14 us -> none  [orthonormal(): lax.linalg.triangular_solve(lower_factor, matrix, left_side=True, lower=T...]
    mul x4 -> x0, other arithmetic: 4.04 us -> none  [wave_deep(): (2.0 * current - earlier + wide_speed * laplace) * inside]
  transfers between devices with their start and end apart: 7 -> 0, of which waited for: 4 -> 0; matrix products, arithmetic and copies ran while one was open for 0% -> 0% of each run, Pallas kernels for 0% -> 0%
where the time goes in v1:
time: 147 us
  Pallas kernels  140 us (95%)
  local copies, waits for them, and re-layouts  6.52 us (4%)
    pallas_call x1, Pallas kernels, body(): pl.pallas_call(functools.partial(kernel, depths, levels), out_shape=(jax....  140 us
    unnamed x8, local copies, waits for them, and re-layouts  6.52 us

profile of v1, /device:TPU:0, one launch (start us, length us, event | category | flops | bytes accessed | tf_op | source)
XLA Modules:
  0.0 147.2 jit_solution(18249702575097009067)
XLA Ops:
  0.6 0.0 copy-start
  0.6 2.1 %copy.9 = bf16[1,64,32,128]{3,1,2,0:T(8,128)(2,1)} copy(bf16[1,64,32,128]{3,2,1,0:T(8,128)(2,1)} %param.3) | data formatting | bytes 1048576 | tf_op args[0]
  2.7 0.0 copy-done
  2.7 1.0 copy.6.sketches
  3.7 140.0 %shard_map.50 = (f32[32,64,128]{2,1,0:T(8,128)}, f32[64,64]{1,0:T(8,128)}) custom-call(bf16[32,64,128]{2,1,0:T(8,128)(2,1)} %bitcast.7, f32[32,128]{1,0:T(8,128)} %speed.1, f32[8,128,64]{2,1,0:T(8,128)} %copy.6.sketches), custom_call_target="tpu_custom_call" | custom-call | tf_op jit(solution)/shard_map/pallas_call | solution.py:340
  143.8 0.0 copy-start.1
  143.8 2.8 %copy.7 = f32[64,32,128]{2,1,0:T(8,128)} copy(f32[64,32,128]{2,0,1:T(8,128)} %bitcast.8) | data formatting | bytes 2097152
  146.6 0.0 copy-done.1
  146.6 0.6 copy.11
Async XLA Ops:
  0.6 2.1 %copy-start = (f32[8,128,64]{1,2,0:T(8,128)S(1)}, f32[8,128,64]{1,2,0:T(8,128)}, u32[]{:S(2)}) copy-start(f32[8,128,64]{1,2,0:T(8,128)} %param.5) | copy-start | bytes 786436
  143.8 2.8 %copy-start.1 = (f32[64,64]{1,0:T(8,128)S(1)}, f32[64,64]{1,0:T(8,128)}, u32[]{:S(2)}) copy-start(f32[64,64]{1,0:T(8,128)} %get-tuple-element.5) | copy-start | bytes 49156

commit v2 on v1

--- a/solution.py
+++ b/solution.py
@@ -15,10 +15,27 @@
 NT = (((1,), (1,)), ((), ()))
 TN = (((0,), (0,)), ((), ()))
 PIECES = 4
+WIDTH = 8
 
 
 def mm(a, b, dims=NN):
     return lax.dot_general(a, b, dims, precision=HI, preferred_element_type=jnp.float32)
+
+
+def split(x):
+    top = x.astype(jnp.bfloat16)
+    return top, (x - top.astype(jnp.float32)).astype(jnp.bfloat16)
+
+
+def mm3(a, b, dims=NN):
+    def part(p, q):
+        return lax.dot_general(p, q, dims, preferred_element_type=jnp.float32)
+
+    return part(a[0], b[0]) + (part(a[0], b[1]) + part(a[1], b[0]))
+
+
+def wide(ref, h, d, picked=slice(None)):
+    return jnp.concatenate([ref[h, d + i, picked] for i in range(WIDTH)], axis=1)
 
 
 def inverse_factor(gram):
@@ -29,18 +46,31 @@
     ).astype(jnp.float32)
     a = jnp.concatenate([gram, eye], axis=1)
     blocks = [a[8 * b : 8 * b + 8] for b in range(n // 8)]
-    for k in range(n - 1):
+    for k in range(0, n, 2):
         b0, r = divmod(k, 8)
-        row = blocks[b0][r : r + 1]
-        row = row * (1.0 / row[:, k : k + 1])
-        for b in range((k + 1) // 8, n // 8):
-            col = blocks[b][:, k : k + 1]
+        first, second = blocks[b0][r : r + 1], blocks[b0][r + 1 : r + 2]
+        p, q, s = first[:, k : k + 1], second[:, k : k + 1], second[:, k + 1 : k + 2]
+        if k == n - 2:
+            break
+        scale = 1.0 / (p * s - q * q)
+        row0 = (s * first - q * second) * scale
+        row1 = (p * second - q * first) * scale
+        for b in range((k + 2) // 8, n // 8):
+            col0, col1 = blocks[b][:, k : k + 1], blocks[b][:, k + 1 : k + 2]
             if b == b0:
-                col = jnp.where(rows[:8] > r, col, 0.0)
-            blocks[b] = blocks[b] - col * row
+                below = rows[:8] > r + 1
+                col0, col1 = jnp.where(below, col0, 0.0), jnp.where(below, col1, 0.0)
+            blocks[b] = blocks[b] - (col0 * row0 + col1 * row1)
     a = jnp.concatenate(blocks, axis=0)
-    pivots = jnp.sum(a[:, :n] * eye, axis=1, keepdims=True)
-    return a[:, n:] * (1.0 / jnp.sqrt(pivots))
+    before = jnp.concatenate([a[n - 1 :], a[: n - 1]], axis=0)
+    even = lax.rem(rows, 2) == 0
+    own = jnp.sum(a[:, :n] * eye, axis=1, keepdims=True)
+    shifted = jnp.concatenate([eye[n - 1 :], eye[: n - 1]], axis=0)
+    side = jnp.sum(a[:, :n] * shifted, axis=1, keepdims=True)
+    above = jnp.sum(before[:, :n] * shifted, axis=1, keepdims=True)
+    ratio = jnp.where(even, 0.0, side / jnp.where(even, 1.0, above))
+    value = own - ratio * side
+    return (a[:, n:] - ratio * before[:, n:]) * (1.0 / jnp.sqrt(value))
 
 
 def kernel(
@@ -121,7 +151,7 @@
         for c in halo_copies(1):
             c.start()
 
-    @pl.loop(0, rows)
+    @pl.loop(0, rows, unroll=4)
     def _(d):
         field_a[STEPS + d] = probes[d].astype(jnp.float32)
 
@@ -166,7 +196,7 @@
         source, target = (field_a, field_b) if step % 2 == 0 else (field_b, field_a)
         last = step == STEPS - 1
 
-        @pl.loop(step + 1, 2 * STEPS + rows - step - 1)
+        @pl.loop(step + 1, 2 * STEPS + rows - step - 1, unroll=2)
         def _(d):
             older = source[d] if step == 0 else target[d]
             new = update(d, source, older)
@@ -194,11 +224,11 @@
         c.wait()
 
     def gram_body(d, total):
-        x = pairs[0, d]
-        return total + mm(x, x, NT)
+        x = split(wide(pairs, 0, d * WIDTH))
+        return total + mm3(x, x, NT)
 
     zero = jnp.zeros((2 * rank, 2 * rank), jnp.float32)
-    gram = lax.fori_loop(0, rows, gram_body, zero)
+    gram = lax.fori_loop(0, rows // WIDTH, gram_body, zero)
 
     def sum_copy(h, j):
         other = lax.rem(depth + j, depths)
@@ -245,9 +275,13 @@
         own_bit = bit(h)
         own = pl.ds(pl.multiple_of(own_bit * rank, rank), rank)
 
-        @pl.loop(0, rows)
-        def _(d):
-            pairs[h, d, own] = mm(mixer, pairs[h - 1, d])
+        parts = split(mixer)
+
+        @pl.loop(0, rows // WIDTH)
+        def _(i):
+            out = mm3(parts, split(wide(pairs, h - 1, i * WIDTH)))
+            for w in range(WIDTH):
+                pairs[h, i * WIDTH + w, own] = out[:, w * cells : (w + 1) * cells]
 
         per = rows // 2 // PIECES
         half = rows // 2
@@ -286,11 +320,12 @@
             forward_copy(i).wait()
 
         def cross_body(d, total):
-            y = pairs[h, d]
-            r = pairs[0, d, mine]
-            return total + mm(y, jnp.concatenate([y[rank:], r], axis=0), NT)
-
-        cross = lax.fori_loop(0, rows, cross_body, zero)
+            y = split(wide(pairs, h, d * WIDTH))
+            r = split(wide(pairs, 0, d * WIDTH, mine))
+            right = [jnp.concatenate([p[rank:], q], axis=0) for p, q in zip(y, r)]
+            return total + mm3(y, right, NT)
+
+        cross = lax.fori_loop(0, rows // WIDTH, cross_body, zero)
         value = jnp.concatenate(
             [
                 cross[:rank, :rank],
@@ -312,9 +347,13 @@
         high_part = jnp.where(own_bit == 0, other, projected)
         projected = mm(mixer, jnp.concatenate([low_part, high_part], axis=0))
 
-    @pl.loop(0, rows)
-    def _(d):
-        basis[d] = mm(mixer, pairs[levels - 1, d])
+    parts = split(mixer)
+
+    @pl.loop(0, rows // WIDTH)
+    def _(i):
+        out = mm3(parts, split(wide(pairs, levels - 1, i * WIDTH)))
+        for w in range(WIDTH):
+            basis[i * WIDTH + w] = out[:, w * cells : (w + 1) * cells]
 
     cores[...] = projected * (1.0 / math.sqrt(rank))
 

time: 147 us -> 105 us (0.71)
  Pallas kernels: 140 us -> 98 us
    pallas_call x1, Pallas kernels: 140 us -> 98 us  [body(): pl.pallas_call(functools.partial(kernel, depths, levels), out_shape=(jax....]
where the time goes in v2:
time: 105 us
  Pallas kernels  98 us (93%)
  local copies, waits for them, and re-layouts  6.52 us (6%)
    pallas_call x1, Pallas kernels, body(): pl.pallas_call(functools.partial(kernel, depths, levels), out_shape=(jax....  98 us
    unnamed x8, local copies, waits for them, and re-layouts  6.52 us

profile of v2, /device:TPU:0, one launch (start us, length us, event | category | flops | bytes accessed | tf_op | source)
XLA Modules:
  0.0 105.2 jit_solution(3427819830045407935)
XLA Ops:
  0.6 0.0 copy-start
  0.6 2.1 %copy.9 = bf16[1,64,32,128]{3,1,2,0:T(8,128)(2,1)} copy(bf16[1,64,32,128]{3,2,1,0:T(8,128)(2,1)} %param.3) | data formatting | bytes 1048576 | tf_op args[0]
  2.7 0.0 copy-done
  2.7 1.0 copy.6.sketches
  3.7 98.0 %shard_map.50 = (f32[32,64,128]{2,1,0:T(8,128)}, f32[64,64]{1,0:T(8,128)}) custom-call(bf16[32,64,128]{2,1,0:T(8,128)(2,1)} %bitcast.7, f32[32,128]{1,0:T(8,128)} %speed.1, f32[8,128,64]{2,1,0:T(8,128)} %copy.6.sketches), custom_call_target="tpu_custom_call" | custom-call | tf_op jit(solution)/shard_map/pallas_call | solution.py:379
  101.7 0.0 copy-start.1
  101.8 2.8 %copy.7 = f32[64,32,128]{2,1,0:T(8,128)} copy(f32[64,32,128]{2,0,1:T(8,128)} %bitcast.8) | data formatting | bytes 2097152
  104.6 0.0 copy-done.1
  104.6 0.6 copy.11
Async XLA Ops:
  0.6 2.1 %copy-start = (f32[8,128,64]{1,2,0:T(8,128)S(1)}, f32[8,128,64]{1,2,0:T(8,128)}, u32[]{:S(2)}) copy-start(f32[8,128,64]{1,2,0:T(8,128)} %param.5) | copy-start | bytes 786436
  101.7 2.8 %copy-start.1 = (f32[64,64]{1,0:T(8,128)S(1)}, f32[64,64]{1,0:T(8,128)}, u32[]{:S(2)}) copy-start(f32[64,64]{1,0:T(8,128)} %get-tuple-element.5) | copy-start | bytes 49156

commit v3 on v2

--- a/solution.py
+++ b/solution.py
@@ -14,7 +14,7 @@
 NN = (((1,), (0,)), ((), ()))
 NT = (((1,), (1,)), ((), ()))
 TN = (((0,), (0,)), ((), ()))
-PIECES = 4
+PIECES = 2
 WIDTH = 8
 
 
@@ -94,8 +94,6 @@
     speed_recv,
     pair_send,
     pair_recv,
-    fwd_send,
-    fwd_recv,
     sum_send,
     sum_recv,
 ):
@@ -211,8 +209,8 @@
             pltpu.make_async_remote_copy(
                 src_ref=pairs.at[h, :, own],
                 dst_ref=pairs.at[h, :, own],
-                send_sem=pair_send.at[h, 0],
-                recv_sem=pair_recv.at[h, 0],
+                send_sem=pair_send.at[h, 0, 0],
+                recv_sem=pair_recv.at[h, 0, 0],
                 device_id=(peer(h), depth),
                 device_id_type=MESH,
             )
@@ -276,48 +274,52 @@
         own = pl.ds(pl.multiple_of(own_bit * rank, rank), rank)
 
         parts = split(mixer)
-
-        @pl.loop(0, rows // WIDTH)
-        def _(i):
-            out = mm3(parts, split(wide(pairs, h - 1, i * WIDTH)))
-            for w in range(WIDTH):
-                pairs[h, i * WIDTH + w, own] = out[:, w * cells : (w + 1) * cells]
-
-        per = rows // 2 // PIECES
-        half = rows // 2
-
-        def piece_copy(i):
-            at = pl.ds(me * half + i * per, per)
+        part_rows = rows // 2**h
+        per = part_rows // PIECES
+        got = pl.ds(pl.multiple_of((1 - own_bit) * rank, rank), rank)
+
+        def part_at(mask, i):
+            part = 0
+            for b in range(h):
+                part += 2**b * (1 - bit(b) if mask >> b & 1 else bit(b))
+            return pl.ds(part * part_rows + i * per, per)
+
+        def part_copy(mask, i):
+            low = mask & -mask
+            at = part_at(mask - low, i)
+            lanes = got if mask else own
             return pltpu.make_async_remote_copy(
-                src_ref=pairs.at[h, at, own],
-                dst_ref=pairs.at[h, at, own],
-                send_sem=pair_send.at[h, i],
-                recv_sem=pair_recv.at[h, i],
-                device_id=(peer(h), depth),
+                src_ref=pairs.at[h, at, lanes],
+                dst_ref=pairs.at[h, at, lanes],
+                send_sem=pair_send.at[h, mask, i],
+                recv_sem=pair_recv.at[h, mask, i],
+                device_id=(peer(low.bit_length() - 1 if mask else h), depth),
                 device_id_type=MESH,
             )
 
-        got = pl.ds(pl.multiple_of((1 - own_bit) * rank, rank), rank)
-
-        def forward_copy(i):
-            at = pl.ds(me * half + i * per, per)
-            return pltpu.make_async_remote_copy(
-                src_ref=pairs.at[h, at, got],
-                dst_ref=pairs.at[h, at, got],
-                send_sem=fwd_send.at[h, i],
-                recv_sem=fwd_recv.at[h, i],
-                device_id=(peer(0), depth),
-                device_id_type=MESH,
-            )
-
-        for i in range(PIECES):
-            piece_copy(i).start()
-        for i in range(PIECES):
-            piece_copy(i).wait_recv()
-            forward_copy(i).start()
-        for i in range(PIECES):
-            piece_copy(i).wait_send()
-            forward_copy(i).wait()
+        chunks = rows // WIDTH
+        ahead = max(1, part_rows // WIDTH)
+        first = part_at(0, 0).start // WIDTH
+        for t in range(chunks):
+            at = lax.rem(first + t, chunks) * WIDTH
+            out = mm3(parts, split(wide(pairs, h - 1, at)))
+            for w in range(WIDTH):
+                pairs[h, at + w, own] = out[:, w * cells : (w + 1) * cells]
+            if per == WIDTH and t < PIECES:
+                part_copy(0, t).start()
+            elif per != WIDTH and t == ahead - 1:
+                for i in range(PIECES):
+                    part_copy(0, i).start()
+        masks = sorted(range(2**h), key=lambda m: (m.bit_count(), -m))
+        for mask in masks:
+            low = mask & -mask if mask else 2**h
+            for i in range(PIECES):
+                part_copy(mask, i).wait_recv()
+                for b in reversed(range(low.bit_length() - 1)):
+                    part_copy(mask + 2**b, i).start()
+        for mask in masks:
+            for i in range(PIECES):
+                part_copy(mask, i).wait_send()
 
         def cross_body(d, total):
             y = split(wide(pairs, h, d * WIDTH))
@@ -396,10 +398,8 @@
             dma((2,)),
             dma((2,)),
             dma((2,)),
-            dma((levels, PIECES)),
-            dma((levels, PIECES)),
-            dma((levels, PIECES)),
-            dma((levels, PIECES)),
+            dma((levels, 2 ** (levels - 1), PIECES)),
+            dma((levels, 2 ** (levels - 1), PIECES)),
             dma((levels, depths)),
             dma((levels, depths)),
         ],

time: 105 us -> 102 us (0.971)
  Pallas kernels: 98 us -> 95 us
    pallas_call x1, Pallas kernels: 98 us -> 95 us  [body(): pl.pallas_call(functools.partial(kernel, depths, levels), out_shape=(jax....]
where the time goes in v3:
time: 102 us
  Pallas kernels  95 us (93%)
  local copies, waits for them, and re-layouts  6.52 us (6%)
    pallas_call x1, Pallas kernels, body(): pl.pallas_call(functools.partial(kernel, depths, levels), out_shape=(jax....  95 us
    unnamed x8, local copies, waits for them, and re-layouts  6.52 us

profile of v3, /device:TPU:0, one launch (start us, length us, event | category | flops | bytes accessed | tf_op | source)
XLA Modules:
  0.0 102.2 jit_solution(2639954477550345337)
XLA Ops:
  0.6 0.0 copy-start
  0.6 2.1 %copy.9 = bf16[1,64,32,128]{3,1,2,0:T(8,128)(2,1)} copy(bf16[1,64,32,128]{3,2,1,0:T(8,128)(2,1)} %param.3) | data formatting | bytes 1048576 | tf_op args[0]
  2.7 0.0 copy-done
  2.7 1.0 copy.6.sketches
  3.7 95.0 %shard_map.50 = (f32[32,64,128]{2,1,0:T(8,128)}, f32[64,64]{1,0:T(8,128)}) custom-call(bf16[32,64,128]{2,1,0:T(8,128)(2,1)} %bitcast.7, f32[32,128]{1,0:T(8,128)} %speed.1, f32[8,128,64]{2,1,0:T(8,128)} %copy.6.sketches), custom_call_target="tpu_custom_call" | custom-call | tf_op jit(solution)/shard_map/pallas_call | solution.py:381
  98.8 0.0 copy-start.1
  98.8 2.8 %copy.7 = f32[64,32,128]{2,1,0:T(8,128)} copy(f32[64,32,128]{2,0,1:T(8,128)} %bitcast.8) | data formatting | bytes 2097152
  101.6 0.0 copy-done.1
  101.6 0.6 copy.11
Async XLA Ops:
  0.6 2.1 %copy-start = (f32[8,128,64]{1,2,0:T(8,128)S(1)}, f32[8,128,64]{1,2,0:T(8,128)}, u32[]{:S(2)}) copy-start(f32[8,128,64]{1,2,0:T(8,128)} %param.5) | copy-start | bytes 786436
  98.8 2.8 %copy-start.1 = (f32[64,64]{1,0:T(8,128)S(1)}, f32[64,64]{1,0:T(8,128)}, u32[]{:S(2)}) copy-start(f32[64,64]{1,0:T(8,128)} %get-tuple-element.5) | copy-start | bytes 49156
